TPU v7x, 32 devices: a whole 2x2x4 slice. The times are simulated.
32 devices in a mesh: chan: 16 (over z, x, core), tm: 2 (over y).
Axes of the slice: x: 2, y: 2, z: 4, core: 2. Of those that a mesh axis runs over, the one named last changes fastest.
Arguments:
- volt: bfloat16 [2, 64, 2048, 512], P(None, None, ('chan', 'tm')), may hold values from -40 to 40
- windows: int32 [64, 2], P('chan'), may hold values from 0 to 2048, as said below
- start_basis: float32 [2, 64, 8, 512], P(None, 'chan'), may hold values from -6 to 6
- positions: float32 [2, 512], replicated, may hold values from -16 to 16
- pointing: float32 [2, 1024], replicated, may hold values from -0.7 to 0.7
- beam_dir: int32 [1024], replicated, may hold values from 0 to 1023, each once
Outputs:
- power: float32 [64, 1024], P('chan', 'tm')
Inputs may be any that keep to these rules, and one draw needn't show every extreme that they name: `windows`: each row holds a channel's first window sample and one past its last; every window holds 1024 samples or more. `beam_dir`: each table entry is named by exactly one beam.
All inputs are finite; a program needn't handle non-finite values.
Results may differ from a plain program's by a relative error of at most 0.0024.
Values may be sent and summed in bfloat16 or wider, within the bound.
No kernel may reach another device: no remote copies, remote signals or barrier semaphores. Data moves between devices by JAX's collectives and lax.ppermute only.
A program may use at most 128 MiB of HBM per device.

v0:
```python
import math
import jax
import jax.numpy as jnp
from jax import lax
from jax.sharding import PartitionSpec as P

ITERS = 6
EPS = 1e-06
TWO_PI = 2.0 * math.pi


def orthonormal(real_part, imag_part):
    number = real_part.shape[-2]
    base_real = []
    base_imag = []
    for column in range(number):
        vec_real = real_part[..., column, :]
        vec_imag = imag_part[..., column, :]
        for earlier in range(column):
            prev_real = base_real[earlier]
            prev_imag = base_imag[earlier]
            coef_real = jnp.sum(prev_real * vec_real + prev_imag * vec_imag, axis=-1, keepdims=True)
            coef_imag = jnp.sum(prev_real * vec_imag - prev_imag * vec_real, axis=-1, keepdims=True)
            vec_real = vec_real - (coef_real * prev_real - coef_imag * prev_imag)
            vec_imag = vec_imag - (coef_real * prev_imag + coef_imag * prev_real)
        inverse = lax.rsqrt(
            jnp.sum(vec_real * vec_real + vec_imag * vec_imag, axis=-1, keepdims=True) + EPS
        )
        base_real.append(vec_real * inverse)
        base_imag.append(vec_imag * inverse)
    return (jnp.stack(base_real, axis=-2), jnp.stack(base_imag, axis=-2))


def fdot(left, right):
    return jnp.dot(left, right, preferred_element_type=jnp.float32)


def fsum(form, left, right):
    return jnp.einsum(form, left, right, preferred_element_type=jnp.float32)


def channel_power(volt_real, volt_imag, base_real, base_imag, freq, direction, positions):
    low_real = base_real.astype(jnp.bfloat16)
    low_imag = base_imag.astype(jnp.bfloat16)
    full_real = (fdot(volt_real, low_real.T) + fdot(volt_imag, low_imag.T)).astype(jnp.bfloat16)
    full_imag = (fdot(volt_imag, low_real.T) - fdot(volt_real, low_imag.T)).astype(jnp.bfloat16)
    removed_real = fdot(full_real, low_real) - fdot(full_imag, low_imag)
    removed_imag = fdot(full_real, low_imag) + fdot(full_imag, low_real)
    clean_real = (volt_real.astype(jnp.float32) - removed_real).astype(jnp.bfloat16)
    clean_imag = (volt_imag.astype(jnp.float32) - removed_imag).astype(jnp.bfloat16)
    phase = (
        TWO_PI
        * freq
        * (
            positions[0][:, None] * direction[0][None, :]
            + positions[1][:, None] * direction[1][None, :]
        )
    )
    steer_real = jnp.cos(phase).astype(jnp.bfloat16)
    steer_imag = jnp.sin(phase).astype(jnp.bfloat16)
    beam_real = fdot(clean_real, steer_real) + fdot(clean_imag, steer_imag)
    beam_imag = fdot(clean_imag, steer_real) - fdot(clean_real, steer_imag)
    return jnp.sum(beam_real * beam_real + beam_imag * beam_imag, axis=0)


def body(volt, windows, start_basis, positions, pointing, beam_dir):
    parts, channels_all, rows_in, stations = volt.shape
    n_chan = lax.axis_size("chan")
    n_time = lax.axis_size("tm")
    chan_dev = channels_all // n_chan
    chan_at = lax.axis_index("chan")
    time_at = lax.axis_index("tm")
    total_time = rows_in * n_chan * n_time
    per_device = chan_dev // n_time
    blocks = volt.reshape(parts, n_chan * n_time, per_device, rows_in, stations)
    moved = lax.all_to_all(blocks, ("chan", "tm"), split_axis=1, concat_axis=3, tiled=True)
    local = moved.reshape(parts, per_device, total_time, stations)
    sample_at = jnp.arange(total_time, dtype=jnp.int32)
    first_channel = chan_at * chan_dev + time_at * per_device
    own_windows = lax.dynamic_slice_in_dim(windows, time_at * per_device, per_device, 0)
    own_basis = lax.dynamic_slice_in_dim(start_basis, time_at * per_device, per_device, 1)
    volt_real = local[0]
    volt_imag = local[1]
    window_mask = (
        (sample_at[None, :] >= own_windows[:, 0:1]) & (sample_at[None, :] < own_windows[:, 1:2])
    ).astype(jnp.float32)
    base_real, base_imag = orthonormal(own_basis[0], own_basis[1])
    for iteration in range(ITERS):
        low_real = base_real.astype(jnp.bfloat16)
        low_imag = base_imag.astype(jnp.bfloat16)
        proj_real = fsum("cts,cks->ctk", volt_real, low_real) + fsum(
            "cts,cks->ctk", volt_imag, low_imag
        )
        proj_imag = fsum("cts,cks->ctk", volt_imag, low_real) - fsum(
            "cts,cks->ctk", volt_real, low_imag
        )
        proj_real = (proj_real * window_mask[:, :, None]).astype(jnp.bfloat16)
        proj_imag = (proj_imag * window_mask[:, :, None]).astype(jnp.bfloat16)
        image_real = fsum("ctk,cts->cks", proj_real, volt_real) - fsum(
            "ctk,cts->cks", proj_imag, volt_imag
        )
        image_imag = fsum("ctk,cts->cks", proj_real, volt_imag) + fsum(
            "ctk,cts->cks", proj_imag, volt_real
        )
        base_real, base_imag = orthonormal(image_real, image_imag)
    direction = jnp.take(pointing, beam_dir, axis=1)
    channel_ids = first_channel + jnp.arange(volt_real.shape[0], dtype=jnp.int32)

    def one_channel(inputs):
        chan_real, chan_imag, basis_re, basis_im, channel = inputs
        freq = 1.0 + channel.astype(jnp.float32) / channels_all
        return channel_power(chan_real, chan_imag, basis_re, basis_im, freq, direction, positions)

    partial_power = lax.map(one_channel, (volt_real, volt_imag, base_real, base_imag, channel_ids))
    scaled = partial_power / (total_time * stations)
    return lax.all_to_all(scaled, "tm", split_axis=1, concat_axis=0, tiled=True)


def solution(mesh):
    return jax.shard_map(
        body,
        mesh=mesh,
        in_specs=(
            P(None, None, ("chan", "tm"), None),
            P("chan", None),
            P(None, "chan", None, None),
            P(),
            P(),
            P(),
        ),
        out_specs=P("chan", "tm"),
        check_vma=False,
    )
```

profile of v0, /device:TPU:2, one launch (start us, length us, event | category | flops | bytes accessed | tf_op | source)
XLA Modules:
  0.0 407.5 jit_solution(8869985679007207590)
XLA Ops:
  0.0 7.7 %copy.2137 = bf16[2,32,2,64,512]{4,3,2,0,1:T(8,128)(2,1)} copy(bf16[2,32,2,64,512]{4,3,2,1,0:T(8,128)(2,1)} %bitcast.1410) | data formatting | bytes 16777216 | tf_op jit(solution)/shard_map/reshape | solution.py:75
  7.7 6.2 %all-to-all-start = ((bf16[2,32,2,64,512]{4,3,2,0,1:T(8,128)(2,1)}), bf16[2,32,2,64,512]{4,3,2,0,1:T(8,128)(2,1)}, u32[]{:S(2)}, u32[]{:S(2)}) async-start(bf16[2,32,2,64,512]{4,3,2,0,1:T(8,128)(2,1)} %copy.2137), calls=%async_computation | async-start | bytes 16777216 | tf_op jit(solution)/shard_map/all_to_all | solution.py:76
  14.2 2.8 gather_fusion
  22.7 175.2 %all-to-all-done = bf16[2,32,2,64,512]{4,3,2,0,1:T(8,128)(2,1)} async-done(((bf16[2,32,2,64,512]{4,3,2,0,1:T(8,128)(2,1)}), bf16[2,32,2,64,512]{4,3,2,0,1:T(8,128)(2,1)}, u32[]{:S(2)}, u32[]{:S(2)}) %all-to-all-start) | async-done | bytes 8388640 | tf_op jit(solution)/shard_map/all_to_all | solution.py:76
  197.9 4.2 %fusion.294 = (bf16[1,1,2,32,64,512]{5,4,2,0,3,1:T(8,128)(2,1)S(1)}, bf16[1,1,2,32,64,512]{5,4,2,0,3,1:T(8,128)(2,1)S(1)}) fusion(bf16[2,1,2,32,64,512]{5,4,2,0,3,1:T(8,128)(2,1)} %bitcast.12), kind=kLoop, calls=%fused_computation.1637 | loop fusion | bytes 16777216 | tf_op jit(solution)/shard_map/slice | solution.py:83
  204.3 1.2 fusion.34
  208.0 1.2 fusion.33
  216.8 1.2 fusion.36
  220.5 1.2 fusion.35
  228.2 1.6 fusion.65
  229.7 1.2 fusion.38
  233.4 1.2 fusion.37
  242.3 1.2 fusion.40
  246.0 1.2 fusion.39
  254.8 1.4 fusion.42
  258.7 1.2 fusion.41
  278.8 117.9 %while.10 = (s32[]{:T(128)}, f32[2,1024]{1,0:T(2,128)S(1)}, bf16[2,2048,512]{2,1,0:T(8,128)(2,1)}, bf16[2,8,512]{2,0,1:T(2,128)(2,1)S(1)}, bf16[2,2048,512]{2,1,...) while((s32[]{:T(128)}, f32[2,1024]{1,0:T(2,128)S(1)}, ...), condition=%wide.region_450.451_spmd, body=%wide.region_448.0_spmd.sunk | while | flops 8755674112 | bytes 126480664 | solution.py:114
  302.9 2.2 fusion.463
  305.1 2.2 fusion.464
  307.4 2.4 fusion.460
  313.5 8.5 %fusion.470 = f32[2048,1024]{1,0:T(8,128)S(1)} fusion(bf16[2048,512]{1,0:T(8,128)(2,1)S(1)} %subtract_convert_fusion.4, f32[1024]{0:T(1024)S(1)} %bitcast.1416, f32[512]{0:T(512)S(1)} %bitcast.1424, f32[1024]{0:T(1024)S(1)} %bitcast.1412, f32[512]{0:T(512)S(1)} %bitcast.1420, f32[]{:T(128)} %bitcast.1358), kind=kOutput, calls=%fused_computation.23.clone.1 | convolution fusion | flops 2150105088 | bytes 10498052 | tf_op jit(solution)/shard_map/while/body/eval_jaxpr/dot_general | solution.py:35
  321.9 8.4 %fusion.467 = f32[2048,1024]{1,0:T(8,128)S(1)} fusion(bf16[2048,512]{1,0:T(8,128)(2,1)S(1)} %subtract_convert_fusion.4, f32[1024]{0:T(1024)S(1)} %bitcast.1417, f32[512]{0:T(512)S(1)} %bitcast.1425, f32[1024]{0:T(1024)S(1)} %bitcast.1413, f32[512]{0:T(512)S(1)} %bitcast.1421, f32[]{:T(128)} %bitcast.1358), kind=kOutput, calls=%fused_computation.21.clone.1 | convolution fusion | flops 2150105088 | bytes 10498052 | tf_op jit(solution)/shard_map/while/body/eval_jaxpr/dot_general | solution.py:35
  330.3 8.4 %fusion.469 = f32[2048,1024]{1,0:T(8,128)S(1)} fusion(bf16[2048,512]{1,0:T(8,128)(2,1)S(1)} %subtract_convert_fusion.5, f32[1024]{0:T(1024)S(1)} %bitcast.1418, f32[512]{0:T(512)S(1)} %bitcast.1426, f32[1024]{0:T(1024)S(1)} %bitcast.1414, f32[512]{0:T(512)S(1)} %bitcast.1422, f32[]{:T(128)} %bitcast.1358), kind=kOutput, calls=%fused_computation.22.clone.1 | convolution fusion | flops 2150105088 | bytes 10498052 | tf_op jit(solution)/shard_map/while/body/eval_jaxpr/dot_general | solution.py:35
  338.8 10.2 %add_reduce_fusion.198 = f32[1024]{0:T(1024)S(1)} fusion(f32[2048,1024]{1,0:T(8,128)S(1)} %fusion.467, f32[2048,1024]{1,0:T(8,128)S(1)} %fusion.469, f32[2048,1024]{1,0:T(8,128)S(1)} %fusion.470, bf16[2048,512]{1,0:T(8,128)(2,1)S(1)} %subtract_convert_fusion.5, f32[1024]{0:T(1024)S(1)} %bitcast.1419, f32[512]{0:T(512)S(1)} %bitcast.1427, ...), kind=kOutput, calls=%fused_computation.1.clone.1 | convolution fusion | flops 2162686976 | bytes 27279364 | tf_op jit(solution)/shard_map/while/body/eval_jaxpr/dot_general | solution.py:35
  350.6 2.2 fusion.463
  352.8 2.2 fusion.464
  355.1 2.4 fusion.460
  361.2 8.5 %fusion.470 = f32[2048,1024]{1,0:T(8,128)S(1)} fusion(bf16[2048,512]{1,0:T(8,128)(2,1)S(1)} %subtract_convert_fusion.4, f32[1024]{0:T(1024)S(1)} %bitcast.1416, f32[512]{0:T(512)S(1)} %bitcast.1424, f32[1024]{0:T(1024)S(1)} %bitcast.1412, f32[512]{0:T(512)S(1)} %bitcast.1420, f32[]{:T(128)} %bitcast.1358), kind=kOutput, calls=%fused_computation.23.clone.1 | convolution fusion | flops 2150105088 | bytes 10498052 | tf_op jit(solution)/shard_map/while/body/eval_jaxpr/dot_general | solution.py:35
  369.6 8.4 %fusion.467 = f32[2048,1024]{1,0:T(8,128)S(1)} fusion(bf16[2048,512]{1,0:T(8,128)(2,1)S(1)} %subtract_convert_fusion.4, f32[1024]{0:T(1024)S(1)} %bitcast.1417, f32[512]{0:T(512)S(1)} %bitcast.1425, f32[1024]{0:T(1024)S(1)} %bitcast.1413, f32[512]{0:T(512)S(1)} %bitcast.1421, f32[]{:T(128)} %bitcast.1358), kind=kOutput, calls=%fused_computation.21.clone.1 | convolution fusion | flops 2150105088 | bytes 10498052 | tf_op jit(solution)/shard_map/while/body/eval_jaxpr/dot_general | solution.py:35
  378.0 8.4 %fusion.469 = f32[2048,1024]{1,0:T(8,128)S(1)} fusion(bf16[2048,512]{1,0:T(8,128)(2,1)S(1)} %subtract_convert_fusion.5, f32[1024]{0:T(1024)S(1)} %bitcast.1418, f32[512]{0:T(512)S(1)} %bitcast.1426, f32[1024]{0:T(1024)S(1)} %bitcast.1414, f32[512]{0:T(512)S(1)} %bitcast.1422, f32[]{:T(128)} %bitcast.1358), kind=kOutput, calls=%fused_computation.22.clone.1 | convolution fusion | flops 2150105088 | bytes 10498052 | tf_op jit(solution)/shard_map/while/body/eval_jaxpr/dot_general | solution.py:35
  386.5 10.2 %add_reduce_fusion.198 = f32[1024]{0:T(1024)S(1)} fusion(f32[2048,1024]{1,0:T(8,128)S(1)} %fusion.467, f32[2048,1024]{1,0:T(8,128)S(1)} %fusion.469, f32[2048,1024]{1,0:T(8,128)S(1)} %fusion.470, bf16[2048,512]{1,0:T(8,128)(2,1)S(1)} %subtract_convert_fusion.5, f32[1024]{0:T(1024)S(1)} %bitcast.1419, f32[512]{0:T(512)S(1)} %bitcast.1427, ...), kind=kOutput, calls=%fused_computation.1.clone.1 | convolution fusion | flops 2162686976 | bytes 27279364 | tf_op jit(solution)/shard_map/while/body/eval_jaxpr/dot_general | solution.py:35
  396.8 9.7 %all_to_all.34 = f32[2,2,512]{2,0,1:T(2,128)S(1)} all-to-all(f32[2,2,512]{2,0,1:T(2,128)S(1)} %bitcast.1428), channel_id=1, replica_groups=mesh['chan'=16,'tm'=2] {'tm'}, dimensions={1} | all-to-all | bytes 16384 | tf_op jit(solution)/shard_map/all_to_all | solution.py:116
  (382 shorter events, 77.6 us)
Async XLA Ops:
  0.0 17.4 %copy-start = (s32[4,2]{0,1:T(2,128)S(1)}, s32[4,2]{0,1:T(2,128)}, u32[]{:S(2)}) copy-start(s32[4,2]{0,1:T(2,128)} %param.9) | copy-start | bytes 100
  7.7 6.2 %copy-start.9 = (f32[2,1024]{1,0:T(2,128)S(1)}, f32[2,1024]{1,0:T(2,128)}, u32[]{:S(2)}) copy-start(f32[2,1024]{1,0:T(2,128)} %param.12) | copy-start | bytes 24580
  7.7 6.5 %copy-start.8 = (s32[1024]{0:T(1024)S(1)}, s32[1024]{0:T(1024)}, u32[]{:S(2)}) copy-start(s32[1024]{0:T(1024)} %param.13) | copy-start | bytes 12292
  7.7 9.8 %copy-start.7 = (f32[2,4,8,512]{3,2,1,0:T(8,128)S(1)}, f32[2,4,8,512]{3,2,1,0:T(8,128)}, u32[]{:S(2)}) copy-start(f32[2,4,8,512]{3,2,1,0:T(8,128)} %param.10) | copy-start | bytes 393220
  7.7 190.2 %all-to-all-start = ((bf16[2,32,2,64,512]{4,3,2,0,1:T(8,128)(2,1)}), bf16[2,32,2,64,512]{4,3,2,0,1:T(8,128)(2,1)}, u32[]{:S(2)}, u32[]{:S(2)}) async-start(bf16[2,32,2,64,512]{4,3,2,0,1:T(8,128)(2,1)} %copy.2137), calls=%async_computation | async-start | bytes 16777216 | tf_op jit(solution)/shard_map/all_to_all | solution.py:76
  202.6 69.8 %copy-start.2 = (bf16[1,1,2,32,64,512]{5,4,3,2,1,0:T(8,128)(2,1)}, bf16[1,1,2,32,64,512]{5,4,3,2,1,0:T(8,128)(2,1)S(1)}, u32[]{:S(2)}) copy-start(bf16[1,1,2,32,64,512]{5,4,3,2,1,0:T(8,128)(2,1)S(1)} %copy.2141) | copy-start | bytes 12582916
  203.1 70.0 %copy-start.4 = (bf16[1,1,2,32,64,512]{5,4,3,2,1,0:T(8,128)(2,1)}, bf16[1,1,2,32,64,512]{5,4,3,2,1,0:T(8,128)(2,1)S(1)}, u32[]{:S(2)}) copy-start(bf16[1,1,2,32,64,512]{5,4,3,2,1,0:T(8,128)(2,1)S(1)} %copy.2138) | copy-start | bytes 12582916
  272.4 6.4 %copy-start.6 = (f32[2,512]{1,0:T(2,128)S(1)}, f32[2,512]{1,0:T(2,128)}, u32[]{:S(2)}) copy-start(f32[2,512]{1,0:T(2,128)} %param.11) | copy-start | bytes 12292
  301.4 8.4 %copy-start.3 = (bf16[2,2048,512]{2,1,0:T(8,128)(2,1)S(1)}, bf16[2,2048,512]{2,1,0:T(8,128)(2,1)}, u32[]{:S(2)}) copy-start(bf16[2,2048,512]{2,1,0:T(8,128)(2,1)} %get-tuple-element.1442) | copy-start | bytes 12582916 | tf_op jit(solution)/shard_map/while
  307.4 3.8 copy-start.5
  349.1 8.4 %copy-start.3 = (bf16[2,2048,512]{2,1,0:T(8,128)(2,1)S(1)}, bf16[2,2048,512]{2,1,0:T(8,128)(2,1)}, u32[]{:S(2)}) copy-start(bf16[2,2048,512]{2,1,0:T(8,128)(2,1)} %get-tuple-element.1442) | copy-start | bytes 12582916 | tf_op jit(solution)/shard_map/while
  355.1 3.8 copy-start.5
  396.8 10.3 %copy-start.1 = (s32[4,2]{0,1:T(2,128)S(1)}, s32[4,2]{0,1:T(2,128)}, u32[]{:S(2)}) copy-start(s32[4,2]{0,1:T(2,128)} %param.9) | copy-start | bytes 100
where the time goes:
time: 411 us; the launch traced here: 407 us
  waiting for transfers between devices  175 us (43%)
  matrix products  137 us (33%)
  other arithmetic  35.5 us (9%)
  loops' own time  24.5 us (6%)
  local copies, waits for them, and re-layouts  18.3 us (4%)
  blocking collectives  9.7 us (2%)
  starting transfers between devices  6.18 us (2%)
    all_to_all x1, waiting for transfers between devices, body(): lax.all_to_all(blocks, ('chan', 'tm'), split_axis=1, concat_axis=3, tiled...  175 us
    dot_general x24, matrix products, fdot(): return jnp.dot(left, right, preferred_element_type=jnp.float32)  92.1 us
    dot_general x48, matrix products, fsum(): return jnp.einsum(form, left, right, preferred_element_type=jnp.float32)  44.9 us
    another operation x1, loops' own time, body(): lax.map(one_channel, (volt_real, volt_imag, base_real, base_imag, channel...  24.5 us
    reduce_sum x56, other arithmetic, orthonormal(): jnp.sum(prev_real * vec_real + prev_imag * vec_imag, axis=-1, keepdims=True)  16.2 us
    reduce_sum x56, other arithmetic, orthonormal(): jnp.sum(vec_real * vec_real + vec_imag * vec_imag, axis=-1, keepdims=True)  10.4 us
    all_to_all x1, blocking collectives, body(): return lax.all_to_all(scaled, 'tm', split_axis=1, concat_axis=0, tiled=True)  9.7 us
  transfers between devices with their start and end apart: 1, of which 1 were waited for; matrix products, arithmetic and copies ran while one was open for 2% of the time, Pallas kernels for 0%

commit v1 on v0

--- a/solution.py
+++ b/solution.py
@@ -73,7 +73,10 @@
     total_time = rows_in * n_chan * n_time
     per_device = chan_dev // n_time
     blocks = volt.reshape(parts, n_chan * n_time, per_device, rows_in, stations)
-    moved = lax.all_to_all(blocks, ("chan", "tm"), split_axis=1, concat_axis=3, tiled=True)
+    size = lax.axis_size(("chan", "tm"))
+    pieces = jnp.stack(jnp.split(blocks, size, axis=1), axis=0)
+    pieces = lax.all_to_all(pieces, ("chan", "tm"), split_axis=0, concat_axis=0)
+    moved = jnp.concatenate(pieces, axis=3)
     local = moved.reshape(parts, per_device, total_time, stations)
     sample_at = jnp.arange(total_time, dtype=jnp.int32)
     first_channel = chan_at * chan_dev + time_at * per_device

time: 411 us -> 424 us (1.032)
  local copies, waits for them, and re-layouts: 18.3 us -> 30.3 us
    unnamed x23 -> x58, local copies, waits for them, and re-layouts: 0.33 us -> 20 us
    reshape x1 -> x0, local copies, waits for them, and re-layouts: 7.72 us -> none  [body(): blocks = volt.reshape(parts, n_chan * n_time, per_device, rows_in, stations)]
where the time goes in v1:
time: 424 us; the launch traced here: 420 us
  waiting for transfers between devices  175 us (41%)
  matrix products  137 us (32%)
  other arithmetic  35.5 us (8%)
  local copies, waits for them, and re-layouts  30.3 us (7%)
  loops' own time  24.5 us (6%)
  blocking collectives  9.72 us (2%)
  starting transfers between devices  6.18 us (1%)
    all_to_all x1, waiting for transfers between devices, body(): pieces = lax.all_to_all(pieces, ('chan', 'tm'), split_axis=0, concat_axis=0)  175 us
    dot_general x24, matrix products, fdot(): return jnp.dot(left, right, preferred_element_type=jnp.float32)  92.3 us
    dot_general x48, matrix products, fsum(): return jnp.einsum(form, left, right, preferred_element_type=jnp.float32)  44.9 us
    another operation x1, loops' own time, body(): lax.map(one_channel, (volt_real, volt_imag, base_real, base_imag, channel...  24.5 us
    unnamed x58, local copies, waits for them, and re-layouts  20 us
    reduce_sum x56, other arithmetic, orthonormal(): jnp.sum(prev_real * vec_real + prev_imag * vec_imag, axis=-1, keepdims=True)  16.2 us
    reduce_sum x56, other arithmetic, orthonormal(): jnp.sum(vec_real * vec_real + vec_imag * vec_imag, axis=-1, keepdims=True)  10.4 us
    all_to_all x1, blocking collectives, body(): return lax.all_to_all(scaled, 'tm', split_axis=1, concat_axis=0, tiled=True)  9.72 us
  transfers between devices with their start and end apart: 1, of which 1 were waited for; matrix products, arithmetic and copies ran while one was open for 2% of the time, Pallas kernels for 0%

profile of v1, /device:TPU:2, one launch (start us, length us, event | category | flops | bytes accessed | tf_op | source)
XLA Modules:
  0.0 419.9 jit_solution(15101036179375383621)
XLA Ops:
  1.1 1.2 constant_dynamic-update-slice_fusion.30
  16.7 3.2 copy-done.6
  19.9 6.2 %all-to-all-start = ((bf16[32,2,1,2,64,512]{5,4,3,2,1,0:T(8,128)(2,1)}), bf16[32,2,1,2,64,512]{5,4,3,2,1,0:T(8,128)(2,1)}, u32[]{:S(2)}, u32[]{:S(2)}) async-start(bf16[32,2,1,2,64,512]{5,4,3,2,1,0:T(8,128)(2,1)} %bitcast.1599), calls=%async_computation | async-start | bytes 16777216 | tf_op jit(solution)/shard_map/all_to_all | solution.py:78
  26.4 2.8 gather_fusion
  34.9 175.2 %all-to-all-done = bf16[32,2,1,2,64,512]{5,4,3,2,1,0:T(8,128)(2,1)} async-done(((bf16[32,2,1,2,64,512]{5,4,3,2,1,0:T(8,128)(2,1)}), bf16[32,2,1,2,64,512]{5,4,3,2,1,0:T(8,128)(2,1)}, u32[]{:S(2)}, u32[]{:S(2)}) %all-to-all-start) | async-done | bytes 8388640 | tf_op jit(solution)/shard_map/all_to_all | solution.py:78
  210.1 4.2 fusion.294
  216.5 1.2 fusion.34
  220.2 1.2 fusion.33
  229.0 1.2 fusion.36
  232.7 1.2 fusion.35
  240.3 1.6 fusion.65
  241.9 1.2 fusion.38
  245.6 1.2 fusion.37
  254.4 1.2 fusion.40
  258.1 1.2 fusion.39
  267.0 1.4 fusion.42
  291.0 118.1 %while.10 = (s32[]{:T(128)}, f32[2,1024]{1,0:T(2,128)S(1)}, bf16[2,2048,512]{2,1,0:T(8,128)(2,1)}, bf16[2,8,512]{2,0,1:T(2,128)(2,1)S(1)}, bf16[2,2048,512]{2,1,...) while((s32[]{:T(128)}, f32[2,1024]{1,0:T(2,128)S(1)}, ...), condition=%wide.region_450.451_spmd, body=%wide.region_448.0_spmd.sunk | while | flops 8755674112 | bytes 126480664 | solution.py:117
  315.0 2.2 fusion.463
  317.3 2.2 fusion.464
  319.5 2.4 fusion.460
  325.7 8.5 %fusion.470 = f32[2048,1024]{1,0:T(8,128)S(1)} fusion(bf16[2048,512]{1,0:T(8,128)(2,1)S(1)} %subtract_convert_fusion.4, f32[1024]{0:T(1024)S(1)} %bitcast.1637, f32[512]{0:T(512)S(1)} %bitcast.1645, f32[1024]{0:T(1024)S(1)} %bitcast.1633, f32[512]{0:T(512)S(1)} %bitcast.1641, f32[]{:T(128)} %bitcast.1547), kind=kOutput, calls=%fused_computation.23.clone.1 | convolution fusion | flops 2150105088 | bytes 10498052 | tf_op jit(solution)/shard_map/while/body/eval_jaxpr/dot_general | solution.py:35
  334.2 8.4 %fusion.467 = f32[2048,1024]{1,0:T(8,128)S(1)} fusion(bf16[2048,512]{1,0:T(8,128)(2,1)S(1)} %subtract_convert_fusion.4, f32[1024]{0:T(1024)S(1)} %bitcast.1638, f32[512]{0:T(512)S(1)} %bitcast.1646, f32[1024]{0:T(1024)S(1)} %bitcast.1634, f32[512]{0:T(512)S(1)} %bitcast.1642, f32[]{:T(128)} %bitcast.1547), kind=kOutput, calls=%fused_computation.21.clone.1 | convolution fusion | flops 2150105088 | bytes 10498052 | tf_op jit(solution)/shard_map/while/body/eval_jaxpr/dot_general | solution.py:35
  342.6 8.4 %fusion.469 = f32[2048,1024]{1,0:T(8,128)S(1)} fusion(bf16[2048,512]{1,0:T(8,128)(2,1)S(1)} %subtract_convert_fusion.5, f32[1024]{0:T(1024)S(1)} %bitcast.1639, f32[512]{0:T(512)S(1)} %bitcast.1647, f32[1024]{0:T(1024)S(1)} %bitcast.1635, f32[512]{0:T(512)S(1)} %bitcast.1643, f32[]{:T(128)} %bitcast.1547), kind=kOutput, calls=%fused_computation.22.clone.1 | convolution fusion | flops 2150105088 | bytes 10498052 | tf_op jit(solution)/shard_map/while/body/eval_jaxpr/dot_general | solution.py:35
  351.0 10.2 %add_reduce_fusion.198 = f32[1024]{0:T(1024)S(1)} fusion(f32[2048,1024]{1,0:T(8,128)S(1)} %fusion.467, f32[2048,1024]{1,0:T(8,128)S(1)} %fusion.469, f32[2048,1024]{1,0:T(8,128)S(1)} %fusion.470, bf16[2048,512]{1,0:T(8,128)(2,1)S(1)} %subtract_convert_fusion.5, f32[1024]{0:T(1024)S(1)} %bitcast.1640, f32[512]{0:T(512)S(1)} %bitcast.1648, ...), kind=kOutput, calls=%fused_computation.1.clone.1 | convolution fusion | flops 2162686976 | bytes 27279364 | tf_op jit(solution)/shard_map/while/body/eval_jaxpr/dot_general | solution.py:35
  362.8 2.2 fusion.463
  365.1 2.2 fusion.464
  367.3 2.4 fusion.460
  373.5 8.5 %fusion.470 = f32[2048,1024]{1,0:T(8,128)S(1)} fusion(bf16[2048,512]{1,0:T(8,128)(2,1)S(1)} %subtract_convert_fusion.4, f32[1024]{0:T(1024)S(1)} %bitcast.1637, f32[512]{0:T(512)S(1)} %bitcast.1645, f32[1024]{0:T(1024)S(1)} %bitcast.1633, f32[512]{0:T(512)S(1)} %bitcast.1641, f32[]{:T(128)} %bitcast.1547), kind=kOutput, calls=%fused_computation.23.clone.1 | convolution fusion | flops 2150105088 | bytes 10498052 | tf_op jit(solution)/shard_map/while/body/eval_jaxpr/dot_general | solution.py:35
  382.0 8.4 %fusion.467 = f32[2048,1024]{1,0:T(8,128)S(1)} fusion(bf16[2048,512]{1,0:T(8,128)(2,1)S(1)} %subtract_convert_fusion.4, f32[1024]{0:T(1024)S(1)} %bitcast.1638, f32[512]{0:T(512)S(1)} %bitcast.1646, f32[1024]{0:T(1024)S(1)} %bitcast.1634, f32[512]{0:T(512)S(1)} %bitcast.1642, f32[]{:T(128)} %bitcast.1547), kind=kOutput, calls=%fused_computation.21.clone.1 | convolution fusion | flops 2150105088 | bytes 10498052 | tf_op jit(solution)/shard_map/while/body/eval_jaxpr/dot_general | solution.py:35
  390.4 8.4 %fusion.469 = f32[2048,1024]{1,0:T(8,128)S(1)} fusion(bf16[2048,512]{1,0:T(8,128)(2,1)S(1)} %subtract_convert_fusion.5, f32[1024]{0:T(1024)S(1)} %bitcast.1639, f32[512]{0:T(512)S(1)} %bitcast.1647, f32[1024]{0:T(1024)S(1)} %bitcast.1635, f32[512]{0:T(512)S(1)} %bitcast.1643, f32[]{:T(128)} %bitcast.1547), kind=kOutput, calls=%fused_computation.22.clone.1 | convolution fusion | flops 2150105088 | bytes 10498052 | tf_op jit(solution)/shard_map/while/body/eval_jaxpr/dot_general | solution.py:35
  398.8 10.2 %add_reduce_fusion.198 = f32[1024]{0:T(1024)S(1)} fusion(f32[2048,1024]{1,0:T(8,128)S(1)} %fusion.467, f32[2048,1024]{1,0:T(8,128)S(1)} %fusion.469, f32[2048,1024]{1,0:T(8,128)S(1)} %fusion.470, bf16[2048,512]{1,0:T(8,128)(2,1)S(1)} %subtract_convert_fusion.5, f32[1024]{0:T(1024)S(1)} %bitcast.1640, f32[512]{0:T(512)S(1)} %bitcast.1648, ...), kind=kOutput, calls=%fused_computation.1.clone.1 | convolution fusion | flops 2162686976 | bytes 27279364 | tf_op jit(solution)/shard_map/while/body/eval_jaxpr/dot_general | solution.py:35
  409.1 9.7 %all_to_all.24 = f32[2,2,512]{2,0,1:T(2,128)S(1)} all-to-all(f32[2,2,512]{2,0,1:T(2,128)S(1)} %bitcast.1649), channel_id=1, replica_groups=mesh['chan'=16,'tm'=2] {'tm'}, dimensions={1} | all-to-all | bytes 16384 | tf_op jit(solution)/shard_map/all_to_all | solution.py:119
  (417 shorter events, 94.2 us)
Async XLA Ops:
  0.0 29.6 %copy-start = (s32[4,2]{0,1:T(2,128)S(1)}, s32[4,2]{0,1:T(2,128)}, u32[]{:S(2)}) copy-start(s32[4,2]{0,1:T(2,128)} %param.9) | copy-start | bytes 100
  0.0 16.2 %copy-start.7 = (bf16[2,64,64,512]{3,2,1,0:T(8,128)(2,1)S(1)}, bf16[2,64,64,512]{3,2,1,0:T(8,128)(2,1)}, u32[]{:S(2)}) copy-start(bf16[2,64,64,512]{3,2,1,0:T(8,128)(2,1)} %param.8) | copy-start | bytes 25165828
  16.7 3.2 copy-start.6
  19.9 6.2 %copy-start.11 = (f32[2,1024]{1,0:T(2,128)S(1)}, f32[2,1024]{1,0:T(2,128)}, u32[]{:S(2)}) copy-start(f32[2,1024]{1,0:T(2,128)} %param.12) | copy-start | bytes 24580
  19.9 6.5 %copy-start.10 = (s32[1024]{0:T(1024)S(1)}, s32[1024]{0:T(1024)}, u32[]{:S(2)}) copy-start(s32[1024]{0:T(1024)} %param.13) | copy-start | bytes 12292
  19.9 9.8 %copy-start.9 = (f32[2,4,8,512]{3,2,1,0:T(8,128)S(1)}, f32[2,4,8,512]{3,2,1,0:T(8,128)}, u32[]{:S(2)}) copy-start(f32[2,4,8,512]{3,2,1,0:T(8,128)} %param.10) | copy-start | bytes 393220
  19.9 190.2 %all-to-all-start = ((bf16[32,2,1,2,64,512]{5,4,3,2,1,0:T(8,128)(2,1)}), bf16[32,2,1,2,64,512]{5,4,3,2,1,0:T(8,128)(2,1)}, u32[]{:S(2)}, u32[]{:S(2)}) async-start(bf16[32,2,1,2,64,512]{5,4,3,2,1,0:T(8,128)(2,1)} %bitcast.1599), calls=%async_computation | async-start | bytes 16777216 | tf_op jit(solution)/shard_map/all_to_all | solution.py:78
  214.8 69.8 %copy-start.2 = (bf16[1,1,2,32,64,512]{5,4,3,2,1,0:T(8,128)(2,1)}, bf16[1,1,2,32,64,512]{5,4,3,2,1,0:T(8,128)(2,1)S(1)}, u32[]{:S(2)}) copy-start(bf16[1,1,2,32,64,512]{5,4,3,2,1,0:T(8,128)(2,1)S(1)} %copy.2265) | copy-start | bytes 12582916
  215.3 69.9 %copy-start.4 = (bf16[1,1,2,32,64,512]{5,4,3,2,1,0:T(8,128)(2,1)}, bf16[1,1,2,32,64,512]{5,4,3,2,1,0:T(8,128)(2,1)S(1)}, u32[]{:S(2)}) copy-start(bf16[1,1,2,32,64,512]{5,4,3,2,1,0:T(8,128)(2,1)S(1)} %copy.2262) | copy-start | bytes 12582916
  284.6 6.4 %copy-start.8 = (f32[2,512]{1,0:T(2,128)S(1)}, f32[2,512]{1,0:T(2,128)}, u32[]{:S(2)}) copy-start(f32[2,512]{1,0:T(2,128)} %param.11) | copy-start | bytes 12292
  313.5 8.4 %copy-start.3 = (bf16[2,2048,512]{2,1,0:T(8,128)(2,1)S(1)}, bf16[2,2048,512]{2,1,0:T(8,128)(2,1)}, u32[]{:S(2)}) copy-start(bf16[2,2048,512]{2,1,0:T(8,128)(2,1)} %get-tuple-element.1442) | copy-start | bytes 12582916 | tf_op jit(solution)/shard_map/while
  319.5 3.8 copy-start.5
  361.3 8.4 %copy-start.3 = (bf16[2,2048,512]{2,1,0:T(8,128)(2,1)S(1)}, bf16[2,2048,512]{2,1,0:T(8,128)(2,1)}, u32[]{:S(2)}) copy-start(bf16[2,2048,512]{2,1,0:T(8,128)(2,1)} %get-tuple-element.1442) | copy-start | bytes 12582916 | tf_op jit(solution)/shard_map/while
  367.3 3.8 copy-start.5
  409.1 10.4 %copy-start.1 = (s32[4,2]{0,1:T(2,128)S(1)}, s32[4,2]{0,1:T(2,128)}, u32[]{:S(2)}) copy-start(s32[4,2]{0,1:T(2,128)} %param.9) | copy-start | bytes 100
